TPU v7x, 32 devices: a whole 2x2x4 slice. The times are simulated.
32 devices in a mesh: grp: 2 (over y), chan: 4 (over z), freq: 2 (over x), section: 2 (over core).
Axes of the slice: x: 2, y: 2, z: 4, core: 2. Of those that a mesh axis runs over, the one named last changes fastest.
Arguments:
- traces: bfloat16 [1024, 128, 384], P(('grp', 'chan'), ('freq', 'section')), parts along dimension 0, may hold values from -6 to 6
- offsets: int32 [256], P(('grp', 'freq', 'section')), parts along dimension 0, may hold values from 0 to 64
- freq_bins: int32 [128], replicated, may hold values from 0 to 128, as said below
- channel_alive: int32 [1024], P(('grp', 'chan')), parts along dimension 0, may hold values 0 or 1
Outputs:
- cross_spectra: bfloat16 [2, 128, 1024, 512], P(None, ('freq', 'section'), ('grp', 'chan')), parts along dimension 2
There are 2 independent parts, one for each index of `grp`. A program takes and returns all parts, laid end to end along the dimension named above; an argument that names none is the same for every part. Nothing has to cross between parts.
Inputs may be any that keep to these rules, and one draw needn't show every extreme that they name: `freq_bins`: distinct and increasing.
All inputs are finite; a program needn't handle non-finite values. No bound on the sum of `channel_alive` on one device may be relied on, other than what follows from the above.
Results may differ from a plain program's by a relative error of at most 0.0025.
The roundings to bfloat16 on the way count: a program that leaves them out, or rounds other values in their place, can miss the bound.
Values may be sent and summed in bfloat16 or wider, within the bound.
A program may use at most 128 MiB of HBM per device.

v0:
```python
import math

import jax
import jax.numpy as jnp
from jax import lax
from jax.sharding import PartitionSpec as P

L = 256
BINS = 128
TAPS = 64
HALF = 64


eps_time = 1e-05
eps_power = 1e-06
low_cut = 0.04
high_cut = 0.42


def swapped(array, axis, stride):
    return lax.ppermute(array, axis, [(i, i ^ 1 << stride) for i in range(lax.axis_size(axis))])


def filter_matrix(offsets, seg_len, length, tap_count):
    sample = jnp.arange(seg_len, dtype=jnp.int32)[None, :, None]
    out_pos = jnp.arange(length, dtype=jnp.int32)[None, None, :]
    lag_steps = sample - offsets[:, None, None] - out_pos
    lag_value = lag_steps.astype(jnp.float32)
    centre = lag_value - (tap_count - 1) / 2.0
    hann_taper = 0.5 - 0.5 * jnp.cos(2.0 * math.pi * lag_value / (tap_count - 1))
    band_pass = 2.0 * high_cut * jnp.sinc(2.0 * high_cut * centre) - 2.0 * low_cut * jnp.sinc(
        2.0 * low_cut * centre
    )
    inside = (lag_steps >= 0) & (lag_steps < tap_count)
    return jnp.where(inside, hann_taper * band_pass, jnp.float32(0.0)).astype(jnp.bfloat16)


def mean_matrix(length, half_width):
    first = jnp.arange(length, dtype=jnp.int32)[:, None]
    second = jnp.arange(length, dtype=jnp.int32)[None, :]
    nearby = (jnp.abs(first - second) <= half_width).astype(jnp.float32)
    return nearby / jnp.sum(nearby, axis=0, keepdims=True)


def dft_table(freq_bins, length):
    positions = jnp.arange(length, dtype=jnp.int32)[:, None]
    angles = (positions * freq_bins[None, :] % length).astype(jnp.float32) * (
        2.0 * math.pi / length
    )
    return jnp.concatenate([jnp.cos(angles), -jnp.sin(angles)], axis=1).astype(jnp.bfloat16)


def whiten(halves, alive):
    values = halves.astype(jnp.float32)
    bin_power = jnp.mean(values[0] * values[0] + values[1] * values[1], axis=1)
    weights = lax.rsqrt(bin_power + eps_power) * alive.astype(jnp.float32)[None, :]
    scaled = values * weights[None, :, None, :]
    return (
        jnp.transpose(scaled, (1, 3, 0, 2))
        .reshape(halves.shape[1], halves.shape[3], -1)
        .astype(jnp.bfloat16)
    )


def cross_block(left_side, blocks, windows):
    product = jnp.einsum("pfik,gfjk->pfigj", left_side, blocks, preferred_element_type=jnp.float32)
    full_shape = product.shape
    scaled = (product * (1.0 / windows)).astype(jnp.bfloat16)
    return scaled.reshape(full_shape[0], full_shape[1], full_shape[2], -1)


def trade_block(blocks, bit_number):
    return swapped(blocks, "chan", bit_number)


def local(traces, offsets, freq_bins, channel_alive):
    block_rows, win_count, seg_len = traces.shape
    fir_matrix = filter_matrix(offsets, seg_len, L, TAPS)
    filtered = jnp.einsum("cws,wsn->wcn", traces, fir_matrix, preferred_element_type=jnp.float32)
    rows = filtered.reshape(-1, L)
    envelope = jnp.dot(
        jnp.abs(rows),
        mean_matrix(L, HALF),
        precision=lax.Precision.HIGHEST,
        preferred_element_type=jnp.float32,
    )
    normed = (rows / (envelope + eps_time)).reshape(filtered.shape).astype(jnp.bfloat16)
    spectra = jnp.einsum(
        "wcn,nj->jwc", normed, dft_table(freq_bins, L), preferred_element_type=jnp.float32
    ).astype(jnp.bfloat16)
    spectra = spectra.reshape(2, BINS, win_count, block_rows)
    bin_spectra = lax.all_to_all(
        spectra, ("freq", "section"), split_axis=1, concat_axis=2, tiled=True
    )
    windows = bin_spectra.shape[2]
    whitened = whiten(bin_spectra, channel_alive)
    real_part = whitened[..., :windows]
    imag_part = whitened[..., windows:]
    left_side = jnp.stack([whitened, jnp.concatenate([imag_part, -real_part], axis=-1)])
    groups = min(8, lax.axis_size("chan"))
    rounds = groups.bit_length() - 1
    bit_order = list(range(rounds))
    my_index = lax.axis_index("chan")
    blocks = whitened[None]
    for bit_number in bit_order:
        partner = trade_block(blocks, bit_number)
        is_lower = my_index >> bit_number & 1 == 0
        blocks = jnp.where(
            is_lower,
            jnp.concatenate([blocks, partner], axis=0),
            jnp.concatenate([partner, blocks], axis=0),
        )
    result = cross_block(left_side, blocks, windows)
    return result


def solution(mesh):
    in_specs = (
        P(("grp", "chan"), ("freq", "section"), None),
        P(("grp", "freq", "section")),
        P(),
        P(("grp", "chan")),
    )
    out_specs = P(None, ("freq", "section"), ("grp", "chan"), None)
    return jax.shard_map(local, mesh=mesh, in_specs=in_specs, out_specs=out_specs, check_vma=False)
```

profile of v0, /device:TPU:0, one launch (start us, length us, event | category | flops | bytes accessed | tf_op | source)
XLA Modules:
  0.0 403.3 jit_solution(11441744537869751902)
XLA Ops:
  0.0 0.1 convert_reduce_fusion
  0.1 0.7 iota_subtract_fusion.1
  0.8 1.3 cosine_convert_fusion
  2.1 83.1 %fusion.39 = f32[32,256,128]{1,2,0:T(8,128)S(1)} fusion(s32[32,384]{1,0:T(8,128)S(1)} %iota_subtract_fusion.1, bf16[128,32,384]{2,1,0:T(8,128)(2,1)} %param.5), kind=kOutput, calls=%fused_computation.64 | convolution fusion | flops 1066401792 | bytes 7389184 | tf_op jit(solution)/shard_map/cws,wsn->wcn/dot_general | solution.py:79
  85.2 0.6 bitcast_abs_fusion
  85.8 3.9 fusion.62
  89.7 0.0 copy-start.1
  89.7 0.7 convolution_convert_fusion
  90.5 2.7 copy.28
  93.1 4.2 %all-to-all-start = ((bf16[2,128,32,128]{3,2,0,1:T(8,128)(2,1)}), bf16[2,128,32,128]{3,2,0,1:T(8,128)(2,1)S(1)}, u32[]{:S(2)}, u32[]{:S(2)}) async-start(bf16[2,128,32,128]{3,2,0,1:T(8,128)(2,1)} %copy.28), calls=%async_computation | async-start | bytes 4194304 | tf_op jit(solution)/shard_map/all_to_all | solution.py:92
  97.4 0.0 copy-done.1
  97.4 25.9 %all-to-all-done = bf16[2,128,32,128]{3,2,0,1:T(8,128)(2,1)S(1)} async-done(((bf16[2,128,32,128]{3,2,0,1:T(8,128)(2,1)}), bf16[2,128,32,128]{3,2,0,1:T(8,128)(2,1)S(1)}, u32[]{:S(2)}, u32[]{:S(2)}) %all-to-all-start) | async-done | bytes 2097184 | tf_op jit(solution)/shard_map/all_to_all | solution.py:92
  123.2 0.4 copy.29
  123.6 0.6 convert_bitcast_fusion
  124.2 0.6 fusion.70
  124.7 0.6 copy.30
  125.4 1.9 fusion.67
  127.3 4.8 %copy.31 = bf16[32,128,2,128]{3,2,1,0:T(2,128)(2,1)S(1)} copy(bf16[32,128,2,128]{1,3,0,2:T(8,128)(2,1)} %bitcast.38) | data formatting | bytes 4194304 | tf_op jit(solution)/shard_map/convert_element_type | solution.py:61
  132.1 2.6 convert_element_type.82
  134.7 2.2 collective-permute-start
  136.9 45.6 %collective-permute-done = bf16[1,32,128,256]{3,2,0,1:T(8,128)(2,1)} collective-permute-done((bf16[1,32,128,256]{3,2,0,1:T(8,128)(2,1)}, bf16[1,32,128,256]{3,2,0,1:T(8,128)(2,1)}, u32[]{:S(2)}, u32[]{:S(2)}) %collective-permute-start) | collective-permute-done | bytes 2097184 | tf_op jit(solution)/shard_map/ppermute | solution.py:21
  182.5 5.7 %fusion.63 = bf16[2,32,128,256]{3,2,0,1:T(8,128)(2,1)} fusion(bf16[1,32,128,256]{3,2,0,1:T(8,128)(2,1)} %convert_element_type.82, bf16[1,32,128,256]{3,2,0,1:T(8,128)(2,1)} %collective-permute-done, pred[]{:T(512)S(6)} %eq.21), kind=kLoop, calls=%fused_computation.89 | loop fusion | flops 6291456 | bytes 8388609 | tf_op jit(solution)/shard_map/jit(_where)/select_n | solution.py:108
  188.3 2.8 collective-permute-start.1
  191.0 2.6 convert_element_type.83
  193.7 0.0 copy-start
  193.7 1.9 fusion.101
  195.6 1.6 maximum_bitcast_fusion
  197.2 173.6 %collective-permute-done.1 = bf16[2,32,128,256]{3,2,0,1:T(8,128)(2,1)} collective-permute-done((bf16[2,32,128,256]{3,2,0,1:T(8,128)(2,1)}, bf16[2,32,128,256]{3,2,0,1:T(8,128)(2,1)}, u32[]{:S(2)}, u32[]{:S(2)}) %collective-permute-start.1) | collective-permute-done | bytes 4194336 | tf_op jit(solution)/shard_map/ppermute | solution.py:21
  370.8 0.0 copy-done
  370.8 10.2 %fusion.58 = bf16[2,32,128,4,128]{2,4,0,3,1:T(8,128)(2,1)} fusion(bf16[2,32,128,256]{3,2,0,1:T(8,128)(2,1)} %collective-permute-done.1, bf16[2,32,128,256]{3,2,0,1:T(8,128)(2,1)} %fusion.63, pred[]{:T(512)S(6)} %eq.20, bf16[1,32,128,256]{3,2,0,1:T(8,128)(2,1)S(1)} %copy-done, bf16[1,32,128,256]{3,2,0,1:T(8,128)(2,1)} %maximum_bitcast_fusion), kind=kOutput, calls=%fused_computation.84 | convolution fusion | flops 2202009600 | bytes 20971520 | tf_op jit(solution)/shard_map/pfik,gfjk->pfigj/dot_general | solution.py:66
  381.0 10.3 %copy.33 = bf16[2,32,128,4,128]{2,4,3,1,0:T(8,128)(2,1)} copy(bf16[2,32,128,4,128]{2,4,0,3,1:T(8,128)(2,1)} %fusion.58) | data formatting | bytes 16777216 | tf_op jit(solution)/shard_map/convert_element_type | solution.py:68
  391.3 12.0 %copy.34 = bf16[2,32,128,512]{3,2,1,0:T(8,128)(2,1)} copy(bf16[2,32,128,512]{2,3,1,0:T(8,128)(2,1)} %bitcast.37) | data formatting | bytes 16777216 | tf_op jit(solution)/shard_map/reshape | solution.py:69
  (2 shorter events, 0.0 us)
Async XLA Ops:
  89.7 7.7 %copy-start.1 = (s32[128]{0:T(128)S(1)}, s32[128]{0:T(128)}, u32[]{:S(2)}) copy-start(s32[128]{0:T(128)} %param.8) | copy-start | bytes 1540
  93.1 30.1 %all-to-all-start = ((bf16[2,128,32,128]{3,2,0,1:T(8,128)(2,1)}), bf16[2,128,32,128]{3,2,0,1:T(8,128)(2,1)S(1)}, u32[]{:S(2)}, u32[]{:S(2)}) async-start(bf16[2,128,32,128]{3,2,0,1:T(8,128)(2,1)} %copy.28), calls=%async_computation | async-start | bytes 4194304 | tf_op jit(solution)/shard_map/all_to_all | solution.py:92
  134.7 47.9 %collective-permute-start = (bf16[1,32,128,256]{3,2,0,1:T(8,128)(2,1)}, bf16[1,32,128,256]{3,2,0,1:T(8,128)(2,1)}, u32[]{:S(2)}, u32[]{:S(2)}) collective-permute-start(bf16[1,32,128,256]{3,2,0,1:T(8,128)(2,1)} %convert_element_type.82), channel_id=1, source_target_pairs={{0,4},{4,0},{8,12},{12,8},{1,5},{5,1},{9,13},{13,9},{2,6},{6,2},{1... | collective-permute-start | bytes 6291464 | tf_op jit(solution)/shard_map/ppermute | solution.py:21
  188.3 182.5 %collective-permute-start.1 = (bf16[2,32,128,256]{3,2,0,1:T(8,128)(2,1)}, bf16[2,32,128,256]{3,2,0,1:T(8,128)(2,1)}, u32[]{:S(2)}, u32[]{:S(2)}) collective-permute-start(bf16[2,32,128,256]{3,2,0,1:T(8,128)(2,1)} %fusion.63), channel_id=1, source_target_pairs={{0,8},{4,12},{8,0},{12,4},{1,9},{5,13},{9,1},{13,5},{2,10},{6,14},... | collective-permute-start | bytes 12582920 | tf_op jit(solution)/shard_map/ppermute | solution.py:21
  193.7 177.2 %copy-start = (bf16[1,32,128,256]{3,2,0,1:T(8,128)(2,1)S(1)}, bf16[1,32,128,256]{3,2,0,1:T(8,128)(2,1)}, u32[]{:S(2)}) copy-start(bf16[1,32,128,256]{3,2,0,1:T(8,128)(2,1)} %convert_element_type.82) | copy-start | bytes 6291460
where the time goes:
time: 404 us; the launch traced here: 403 us
  waiting for transfers between devices  245 us (61%)
  matrix products  97.9 us (24%)
  local copies, waits for them, and re-layouts  36 us (9%)
  other arithmetic  15 us (4%)
  starting transfers between devices  9.2 us (2%)
    ppermute x2, waiting for transfers between devices, swapped(): lax.ppermute(array, axis, [(i, i ^ 1 << stride) for i in range(lax.axis_s...  219 us
    dot_general x1, matrix products, local(): jnp.einsum('cws,wsn->wcn', traces, fir_matrix, preferred_element_type=jnp...  83.1 us
    all_to_all x1, waiting for transfers between devices, local(): lax.all_to_all(spectra, ('freq', 'section'), split_axis=1, concat_axis=2,...  25.9 us
    reshape x1, local copies, waits for them, and re-layouts, cross_block(): return scaled.reshape(full_shape[0], full_shape[1], full_shape[2], -1)  12 us
    convert_element_type x1, local copies, waits for them, and re-layouts, cross_block(): scaled = (product * (1.0 / windows)).astype(jnp.bfloat16)  10.3 us
    dot_general x1, matrix products, cross_block(): jnp.einsum('pfik,gfjk->pfigj', left_side, blocks, preferred_element_type=...  10.2 us
    convert_element_type x3, local copies, waits for them, and re-layouts, whiten(): return jnp.transpose(scaled, (1, 3, 0, 2)).reshape(halves.shape[1], halve...  9.99 us
  transfers between devices with their start and end apart: 3, of which 3 were waited for; matrix products, arithmetic and copies ran while one was open for 2% of the time, Pallas kernels for 0%

commit v1 on v0

v1 whole, which is shorter than its diff:
```python
import functools
import math

import jax
import jax.numpy as jnp
from jax import lax
from jax.experimental import pallas as pl
from jax.experimental.pallas import tpu as pltpu
from jax.sharding import PartitionSpec as P

L = 256
BINS = 128
TAPS = 64
HALF = 64
MAXOFF = 64

eps_time = 1e-05
eps_power = 1e-06
low_cut = 0.04
high_cut = 0.42

MESH = pl.DeviceIdType.MESH
F32 = jnp.float32
BF16 = jnp.bfloat16


def toeplitz(length, depth, tap_count):
    out_pos = jnp.arange(length, dtype=jnp.int32)[:, None]
    sample = jnp.arange(depth, dtype=jnp.int32)[None, :]
    lag_steps = sample - out_pos
    lag_value = lag_steps.astype(F32)
    centre = lag_value - (tap_count - 1) / 2.0
    hann_taper = 0.5 - 0.5 * jnp.cos(2.0 * math.pi * lag_value / (tap_count - 1))
    band_pass = 2.0 * high_cut * jnp.sinc(2.0 * high_cut * centre) - 2.0 * low_cut * jnp.sinc(
        2.0 * low_cut * centre
    )
    inside = (lag_steps >= 0) & (lag_steps < tap_count)
    return jnp.where(inside, hann_taper * band_pass, F32(0.0)).astype(BF16)


def dft_rows(freq_bins, length, owners):
    positions = jnp.arange(length, dtype=jnp.int32)[None, :]
    angles = (positions * freq_bins[:, None] % length).astype(F32) * (2.0 * math.pi / length)
    table = jnp.stack([jnp.cos(angles), -jnp.sin(angles)]).astype(BF16)
    table = table.reshape(2, owners, -1, length)
    return jnp.swapaxes(table, 0, 1).reshape(-1, length)


def spectra_kernel(offsets, x_ref, fir_ref, table_ref, alive_ref, out_ref, seg, acc):
    step = pl.program_id(0)
    batch, _, chans = x_ref.shape
    depth = fir_ref.shape[1]
    rows, wins = table_ref.shape[0], out_ref.shape[0] // table_ref.shape[0]
    shifted = []
    for i in range(batch):
        seg[i] = x_ref[i].astype(F32)
        shifted.append(seg[i, pl.ds(offsets[step * batch + i], depth), :].astype(BF16))
    filtered = jnp.dot(fir_ref[...], jnp.concatenate(shifted, axis=1), preferred_element_type=F32)
    first = lax.broadcasted_iota(jnp.int32, (L, L), 0)
    second = lax.broadcasted_iota(jnp.int32, (L, L), 1)
    band = jnp.where(jnp.abs(first - second) <= HALF, F32(1), F32(0)).astype(BF16)
    size = jnp.abs(filtered)
    high = size.astype(BF16)
    rest = size - high.astype(F32)
    mid = rest.astype(BF16)
    low = (rest - mid.astype(F32)).astype(BF16)
    total = jnp.dot(band, high, preferred_element_type=F32)
    total += jnp.dot(band, mid, preferred_element_type=F32)
    total += jnp.dot(band, low, preferred_element_type=F32)
    place = lax.broadcasted_iota(jnp.int32, (L, 1), 0)
    count = jnp.minimum(place + HALF, L - 1) - jnp.maximum(place - HALF, 0) + 1
    envelope = total * (1.0 / count.astype(F32))
    normed = (filtered / (envelope + eps_time)).astype(BF16)
    spectra = jnp.dot(table_ref[...], normed, preferred_element_type=F32)
    alive = alive_ref[...].astype(F32)
    for i in range(batch):
        acc[pl.ds(step * batch + i, rows, stride=wins), :] = (
            spectra[:, i * chans : (i + 1) * chans] * alive
        )

    @pl.when(step == pl.num_programs(0) - 1)
    def _():
        out_ref[...] = acc[...].astype(BF16)


def gather_kernel(owners, sections, group, spec, gath, put_sem, a2a_send, a2a_recv, up_send, up_recv, dn_send, dn_recv):
    chan = lax.axis_index("chan")
    place = lax.rem(chan, group)
    mine = lax.axis_index("freq") * sections + lax.axis_index("section")

    def other(d):
        q = mine
        for bit in range(d.bit_length()):
            if d >> bit & 1:
                q = q + (1 << bit) - 2 * (1 << bit) * lax.rem(mine // (1 << bit), 2)
        return q

    def peer(d):
        q = other(d)
        return {"freq": q // sections, "section": lax.rem(q, sections)}

    has_up, has_dn = place + 1 < group, place >= 1
    barrier = pltpu.get_barrier_semaphore()
    for d in range(1, owners):
        pl.semaphore_signal(barrier, inc=1, device_id=peer(d), device_id_type=MESH)

    @pl.when(has_up)
    def _():
        pl.semaphore_signal(barrier, inc=1, device_id={"chan": chan + 1}, device_id_type=MESH)

    @pl.when(has_dn)
    def _():
        pl.semaphore_signal(barrier, inc=1, device_id={"chan": chan - 1}, device_id_type=MESH)

    pl.semaphore_wait(barrier, owners - 1 + has_up.astype(jnp.int32) + has_dn.astype(jnp.int32))

    def a2a(d):
        return pltpu.make_async_remote_copy(
            src_ref=spec.at[other(d)],
            dst_ref=gath.at[place, mine],
            send_sem=a2a_send.at[d],
            recv_sem=a2a_recv.at[d],
            device_id=peer(d),
            device_id_type=MESH,
        )

    def hop(k, d, up):
        block = place - k if up else place + k
        source = spec.at[mine] if k == 0 and d == 0 else gath.at[block, other(d)]
        return pltpu.make_async_remote_copy(
            src_ref=source,
            dst_ref=gath.at[block, other(d)],
            send_sem=(up_send if up else dn_send).at[k, d],
            recv_sem=(up_recv if up else dn_recv).at[k, d],
            device_id={"chan": chan + 1 if up else chan - 1},
            device_id_type=MESH,
        )

    def send(k, d, finish=False):
        for up in (True, False):
            there = (place - k >= 0) & has_up if up else (place + k < group) & has_dn

            @pl.when(there)
            def _():
                copy = hop(k, d, up)
                if finish:
                    copy.wait_send()
                else:
                    copy.start()

    put = pltpu.make_async_copy(spec.at[mine], gath.at[place, mine], put_sem)
    send(0, 0)
    for d in range(1, owners):
        a2a(d).start()
    put.start()
    for d in range(1, owners):
        a2a(d).wait_recv()
        send(0, d)
    for k in range(1, group):
        for d in range(owners):
            for up in (True, False):
                comes = place - k >= 0 if up else place + k < group
                goes = has_up if up else has_dn

                @pl.when(comes)
                def _():
                    pltpu.make_async_remote_copy(
                        src_ref=spec.at[mine],
                        dst_ref=gath.at[place - k if up else place + k, other(d)],
                        send_sem=(up_send if up else dn_send).at[k - 1, d],
                        recv_sem=(up_recv if up else dn_recv).at[k - 1, d],
                        device_id={"chan": chan - 1 if up else chan + 1},
                        device_id_type=MESH,
                    ).wait_recv()

                @pl.when(comes & goes)
                def _():
                    hop(k, d, up).start()

    put.wait()
    for d in range(1, owners):
        a2a(d).wait_send()
    for k in range(group - 1):
        for d in range(owners):
            send(k, d, finish=True)


def cross_kernel(place, windows, data, out):
    group, owners, _, batch, wins, chans = data.shape
    mine = place[0]
    for f in range(batch):
        def whitened(b):
            values = data[b, :, :, f].astype(F32)
            values = jnp.swapaxes(values, 0, 1).reshape(2 * owners * wins, chans)
            power = jnp.sum(values * values, axis=0, keepdims=True) * (1.0 / windows)
            return (values * lax.rsqrt(power + eps_power)).astype(BF16)

        right = jnp.concatenate([whitened(b) for b in range(group)], axis=1)
        own = whitened(mine)
        half = owners * wins
        turned = jnp.concatenate([own[half:], -own[:half]], axis=0)
        left = jnp.concatenate([own, turned], axis=1)
        product = lax.dot_general(
            left, right, (((0,), (0,)), ((), ())), preferred_element_type=F32
        )
        scaled = (product * (1.0 / windows)).astype(BF16)
        out[0, f] = scaled[:chans]
        out[1, f] = scaled[chans:]


def local(sizes, traces, offsets, freq_bins, channel_alive):
    chans, wins, seg_len = traces.shape
    owners = sizes["freq"] * sizes["section"]
    group = min(8, sizes["chan"])
    bins = BINS // owners
    rows = 2 * bins * wins
    depth = seg_len - MAXOFF
    batch = 4
    whole = lambda *shape: pl.BlockSpec(shape, lambda *_: (0,) * len(shape))
    spectra = pl.pallas_call(
        spectra_kernel,
        grid_spec=pltpu.PrefetchScalarGridSpec(
            num_scalar_prefetch=1,
            grid=(wins // batch,),
            in_specs=[
                pl.BlockSpec((batch, seg_len, chans), lambda i, _: (i, 0, 0)),
                whole(L, depth),
                whole(2 * BINS, L),
                whole(1, chans),
            ],
            out_specs=whole(2 * BINS * wins, chans),
            scratch_shapes=[
                pltpu.VMEM((batch, seg_len, chans), F32),
                pltpu.VMEM((2 * BINS * wins, chans), F32),
            ],
        ),
        out_shape=jax.ShapeDtypeStruct((2 * BINS * wins, chans), BF16),
        name="spectra",
    )(
        offsets,
        jnp.transpose(traces, (1, 2, 0)),
        toeplitz(L, depth, TAPS),
        dft_rows(freq_bins, L, owners),
        channel_alive.reshape(1, chans),
    )
    dma = pltpu.SemaphoreType.DMA
    gathered = pl.pallas_call(
        functools.partial(gather_kernel, owners, sizes["section"], group),
        in_specs=[pl.BlockSpec(memory_space=pl.ANY)],
        out_specs=pl.BlockSpec(memory_space=pl.ANY),
        out_shape=jax.ShapeDtypeStruct((group, owners, rows, chans), BF16),
        scratch_shapes=[dma, dma((owners,)), dma((owners,))] + [dma((group, owners))] * 4,
        compiler_params=pltpu.CompilerParams(collective_id=0, has_side_effects=True),
        name="gather",
    )(spectra.reshape(owners, rows, chans))
    fold = 2
    place = lax.rem(lax.axis_index("chan"), group).astype(jnp.int32).reshape(1)
    return pl.pallas_call(
        lambda place, data, out: cross_kernel(place, wins * owners, data, out),
        grid_spec=pltpu.PrefetchScalarGridSpec(
            num_scalar_prefetch=1,
            grid=(bins // fold,),
            in_specs=[
                pl.BlockSpec(
                    (group, owners, 2, fold, wins, chans), lambda i, _: (0, 0, 0, i, 0, 0)
                )
            ],
            out_specs=pl.BlockSpec((2, fold, chans, group * chans), lambda i, _: (0, i, 0, 0)),
        ),
        out_shape=jax.ShapeDtypeStruct((2, bins, chans, group * chans), BF16),
        name="cross",
    )(place, gathered.reshape(group, owners, 2, bins, wins, chans))


def solution(mesh):
    in_specs = (
        P(("grp", "chan"), ("freq", "section"), None),
        P(("grp", "freq", "section")),
        P(),
        P(("grp", "chan")),
    )
    out_specs = P(None, ("freq", "section"), ("grp", "chan"), None)
    sizes = dict(mesh.shape)
    return jax.shard_map(
        functools.partial(local, sizes),
        mesh=mesh,
        in_specs=in_specs,
        out_specs=out_specs,
        check_vma=False,
    )
```

time: 404 us -> 181 us (0.45)
  waiting for transfers between devices: 245 us -> 0 us
  Pallas kernels: 0 us -> 170 us
  matrix products: 97.9 us -> 0 us
  local copies, waits for them, and re-layouts: 36 us -> 5.64 us
  other arithmetic: 15 us -> 4.29 us
  starting transfers between devices: 9.2 us -> 0 us
    ppermute x2 -> x0, waiting for transfers between devices: 219 us -> none  [swapped(): lax.ppermute(array, axis, [(i, i ^ 1 << stride) for i in range(lax.axis_s...]
    pallas_call x0 -> x3, Pallas kernels: none -> 170 us  [the longest x1 141 us: local(): pl.pallas_call(functools.partial(gather_kernel, owners, sizes['section'],...]
    dot_general x4 -> x0, matrix products: 97.9 us -> none  [the longest x1 83.1 us: local(): jnp.einsum('cws,wsn->wcn', traces, fir_matrix, preferred_element_type=jnp...]
    all_to_all x1 -> x0, waiting for transfers between devices: 25.9 us -> none  [local(): lax.all_to_all(spectra, ('freq', 'section'), split_axis=1, concat_axis=2,...]
    convert_element_type x5 -> x0, local copies, waits for them, and re-layouts: 21 us -> none  [the longest x1 10.3 us: cross_block(): scaled = (product * (1.0 / windows)).astype(jnp.bfloat16)]
    reshape x2 -> x0, local copies, waits for them, and re-layouts: 14.6 us -> none  [the longest x1 12 us: cross_block(): return scaled.reshape(full_shape[0], full_shape[1], full_shape[2], -1)]
    select_n x1 -> x0, other arithmetic: 5.73 us -> none  [local(): jnp.where(is_lower, jnp.concatenate([blocks, partner], axis=0), jnp.conca...]
    ppermute x2 -> x0, starting transfers between devices: 4.96 us -> none  [swapped(): lax.ppermute(array, axis, [(i, i ^ 1 << stride) for i in range(lax.axis_s...]
  transfers between devices with their start and end apart: 3 -> 0, of which waited for: 3 -> 0; matrix products, arithmetic and copies ran while one was open for 2% -> 0% of each run, Pallas kernels for 0% -> 0%
where the time goes in v1:
time: 181 us; the launch traced here: 180 us
  Pallas kernels  170 us (94%)
  local copies, waits for them, and re-layouts  5.64 us (3%)
  other arithmetic  4.29 us (2%)
    pallas_call x1, Pallas kernels, local(): pl.pallas_call(functools.partial(gather_kernel, owners, sizes['section'],...  141 us
    pallas_call x1, Pallas kernels, local(): pl.pallas_call(lambda place, data, out: cross_kernel(place, wins * owners...  15.3 us
    pallas_call x1, Pallas kernels, local(): pl.pallas_call(spectra_kernel, grid_spec=pltpu.PrefetchScalarGridSpec(num...  13.3 us
    unnamed x1, local copies, waits for them, and re-layouts  4.9 us

profile of v1, /device:TPU:0, one launch (start us, length us, event | category | flops | bytes accessed | tf_op | source)
XLA Modules:
  0.0 179.9 jit_solution(15180301514879042156)
XLA Ops:
  0.0 0.7 mul.113
  0.7 0.6 cosine_convert_fusion
  1.4 0.7 pad_maximum_fusion
  2.0 3.0 %select_convert_fusion.fir_ref = bf16[256,320]{1,0:T(8,128)(2,1)} fusion(), kind=kLoop, calls=%fused_computation.50 | loop fusion | flops 6799360 | bytes 163840 | tf_op jit(solution)/shard_map/convert_element_type | solution.py:38
  5.0 4.9 %copy.5 = bf16[128,32,384]{0,2,1:T(8,128)(2,1)} copy(bf16[128,32,384]{2,1,0:T(8,128)(2,1)} %param.5) | data formatting | bytes 6291456 | tf_op args[0]
  9.9 13.3 %spectra.1 = bf16[8192,128]{1,0:T(8,128)(2,1)} custom-call(s32[32]{0:T(128)} %offsets.1, bf16[32,384,128]{2,1,0:T(8,128)(2,1)} %bitcast.9, bf16[256,320]{1,0:T(8,128)(2,1)} %select_convert_fusion.fir_ref, bf16[256,256]{1,0:T(8,128)(2,1)} %bitcast.11, s32[1,128]{1,0:T(1,128)} %bitcast.12), custom_call_target="tpu_custom_call" | custom-call | tf_op jit(solution)/shard_map/spectra/pallas_call | solution.py:220
  23.3 141.3 %gather.1 = bf16[4,4,2048,128]{3,2,1,0:T(8,128)(2,1)} custom-call(bf16[4,2048,128]{2,1,0:T(8,128)(2,1)} %bitcast.10), custom_call_target="tpu_custom_call" | custom-call | tf_op jit(solution)/shard_map/gather/pallas_call | solution.py:247
  164.6 15.3 %cross.1 = bf16[2,32,128,512]{3,2,1,0:T(8,128)(2,1)} custom-call(s32[1]{0:T(128)} %bitcast.place, bf16[4,4,2,32,32,128]{5,4,3,2,1,0:T(8,128)(2,1)} %bitcast.8), custom_call_target="tpu_custom_call" | custom-call | tf_op jit(solution)/shard_map/cross/pallas_call | solution.py:258

commit v2 on v1

v2 whole, which is shorter than its diff:
```python
import functools
import math

import jax
import jax.numpy as jnp
from jax import lax
from jax.experimental import pallas as pl
from jax.experimental.pallas import tpu as pltpu
from jax.sharding import PartitionSpec as P

L = 256
BINS = 128
TAPS = 64
HALF = 64
MAXOFF = 64

eps_time = 1e-05
eps_power = 1e-06
low_cut = 0.04
high_cut = 0.42

MESH = pl.DeviceIdType.MESH
F32 = jnp.float32
BF16 = jnp.bfloat16


def filter_taps(width, tap_count):
    lag_steps = jnp.arange(width, dtype=jnp.int32)[None, :]
    lag_value = lag_steps.astype(F32)
    centre = lag_value - (tap_count - 1) / 2.0
    hann_taper = 0.5 - 0.5 * jnp.cos(2.0 * math.pi * lag_value / (tap_count - 1))
    band_pass = 2.0 * high_cut * jnp.sinc(2.0 * high_cut * centre) - 2.0 * low_cut * jnp.sinc(
        2.0 * low_cut * centre
    )
    return jnp.where(lag_steps < tap_count, hann_taper * band_pass, F32(0.0))


def dft_rows(freq_bins, length, owners):
    positions = jnp.arange(length, dtype=jnp.int32)[None, :]
    angles = (positions * freq_bins[:, None] % length).astype(F32) * (2.0 * math.pi / length)
    table = jnp.stack([jnp.cos(angles), -jnp.sin(angles)]).astype(BF16)
    table = table.reshape(2, owners, -1, length)
    return jnp.swapaxes(table, 0, 1).reshape(-1, length)


def spectra(offsets, first_win, frames, fir, table, alive, frame, acc):
    wins = frames.shape[1]
    chans, seg_len = frames.shape[0], frames.shape[2]
    rows, batch = table.shape[0], min(8, wins)
    lanes = frame.shape[2]
    for t in range(seg_len // lanes):
        one = frames[:, :, t * lanes : (t + 1) * lanes].astype(F32)
        frame[t] = one.reshape(chans * wins, lanes)
    row = lax.broadcasted_iota(jnp.int32, (L, L), 0)
    column = lax.broadcasted_iota(jnp.int32, (L, L), 1)
    band = jnp.where(jnp.abs(row - column) <= HALF, F32(1), F32(0)).astype(BF16)
    spot = lax.broadcasted_iota(jnp.int32, (L, 1), 0)
    count = jnp.minimum(spot + HALF, L - 1) - jnp.maximum(spot - HALF, 0) + 1
    share = 1.0 / count.astype(F32)
    for base in range(0, wins, batch):
        shifted = []
        for w in range(base, base + batch):
            turn = lax.rem(seg_len - offsets[first_win + w], seg_len)
            one = jnp.concatenate(
                [frame[t, pl.ds(w, chans, stride=wins), :] for t in range(seg_len // lanes)], axis=1
            )
            shifted.append(pltpu.roll(one, turn, 1).astype(BF16))
        filtered = lax.dot_general(
            fir,
            jnp.concatenate(shifted, axis=0),
            (((1,), (1,)), ((), ())),
            preferred_element_type=F32,
        )
        size = jnp.abs(filtered)
        high = size.astype(BF16)
        rest = size - high.astype(F32)
        mid = rest.astype(BF16)
        low = (rest - mid.astype(F32)).astype(BF16)
        total = jnp.dot(band, high, preferred_element_type=F32)
        total += jnp.dot(band, mid, preferred_element_type=F32)
        total += jnp.dot(band, low, preferred_element_type=F32)
        normed = (filtered / (total * share + eps_time)).astype(BF16)
        bands = jnp.dot(table, normed, preferred_element_type=F32)
        for i in range(batch):
            acc[pl.ds(base + i, rows, stride=wins), :] = (
                bands[:, i * chans : (i + 1) * chans] * alive
            )


def gather_kernel(
    owners, sections, group,
    offsets, traces, taps, table, alive, gath,
    frames, frame, acc, spec, load_sem, put_sem,
    a2a_send, a2a_recv, up_send, up_recv, dn_send, dn_recv,
):
    chunks, _, wins, seg_len = frames.shape
    loads = [
        pltpu.make_async_copy(
            traces.at[:, pl.ds(j * wins, wins), :], frames.at[j], load_sem.at[j]
        )
        for j in range(chunks)
    ]
    for load in loads:
        load.start()
    chan = lax.axis_index("chan")
    place = lax.rem(chan, group)
    mine = lax.axis_index("freq") * sections + lax.axis_index("section")

    def other(d):
        q = mine
        for bit in range(d.bit_length()):
            if d >> bit & 1:
                q = q + (1 << bit) - 2 * (1 << bit) * lax.rem(mine // (1 << bit), 2)
        return q

    def peer(d):
        q = other(d)
        return {"freq": q // sections, "section": lax.rem(q, sections)}

    has_up, has_dn = place + 1 < group, place >= 1
    barrier = pltpu.get_barrier_semaphore()
    for d in range(1, owners):
        pl.semaphore_signal(barrier, inc=1, device_id=peer(d), device_id_type=MESH)

    @pl.when(has_up)
    def _():
        pl.semaphore_signal(barrier, inc=1, device_id={"chan": chan + 1}, device_id_type=MESH)

    @pl.when(has_dn)
    def _():
        pl.semaphore_signal(barrier, inc=1, device_id={"chan": chan - 1}, device_id_type=MESH)

    def a2a(d, j):
        return pltpu.make_async_remote_copy(
            src_ref=spec.at[j, other(d)],
            dst_ref=gath.at[place, mine, j],
            send_sem=a2a_send.at[d, j],
            recv_sem=a2a_recv.at[d, j],
            device_id=peer(d),
            device_id_type=MESH,
        )

    def own(j, up):
        return pltpu.make_async_remote_copy(
            src_ref=spec.at[j, mine],
            dst_ref=gath.at[place, mine, j],
            send_sem=(up_send if up else dn_send).at[0, 0, j],
            recv_sem=(up_recv if up else dn_recv).at[0, 0, j],
            device_id={"chan": chan + 1 if up else chan - 1},
            device_id_type=MESH,
        )

    def hop(k, d, up):
        block = place - k if up else place + k
        return pltpu.make_async_remote_copy(
            src_ref=gath.at[block, other(d)],
            dst_ref=gath.at[block, other(d)],
            send_sem=(up_send if up else dn_send).at[k, d, 0],
            recv_sem=(up_recv if up else dn_recv).at[k, d, 0],
            device_id={"chan": chan + 1 if up else chan - 1},
            device_id_type=MESH,
        )

    def arrival(k, d, j, up):
        block = place - k if up else place + k
        ref = gath.at[block, mine, j] if k == 1 and d == 0 else gath.at[block, other(d)]
        return pltpu.make_async_remote_copy(
            src_ref=ref,
            dst_ref=ref,
            send_sem=(up_send if up else dn_send).at[k - 1, d, j],
            recv_sem=(up_recv if up else dn_recv).at[k - 1, d, j],
            device_id={"chan": chan - 1 if up else chan + 1},
            device_id_type=MESH,
        )

    def put(j):
        return pltpu.make_async_copy(spec.at[j, mine], gath.at[place, mine, j], put_sem.at[j])

    ways = ((True, has_up), (False, has_dn))
    padded = jnp.broadcast_to(taps[...], (L, seg_len))
    fir = pltpu.roll(padded, 0, 1, stride=1, stride_axis=0).astype(BF16)
    lives = alive[...].astype(F32)
    for j in range(chunks):
        loads[j].wait()
        spectra(offsets, j * wins, frames[j], fir, table[...], lives, frame, acc)
        spec[j] = acc[...].astype(BF16).reshape(spec.shape[1:])
        if j == 0:
            pl.semaphore_wait(
                barrier, owners - 1 + has_up.astype(jnp.int32) + has_dn.astype(jnp.int32)
            )
        for up, goes in ways:

            @pl.when(goes)
            def _():
                own(j, up).start()

        for d in range(1, owners):
            a2a(d, j).start()
        put(j).start()
    for d in range(1, owners):
        for j in range(chunks):
            a2a(d, j).wait_recv()
        for up, goes in ways:

            @pl.when(goes)
            def _():
                hop(0, d, up).start()

    for k in range(1, group):
        for d in range(owners):
            for up, goes in ways:
                comes = place - k >= 0 if up else place + k < group

                @pl.when(comes)
                def _():
                    for j in range(chunks if k == 1 and d == 0 else 1):
                        arrival(k, d, j, up).wait_recv()

                @pl.when(comes & goes)
                def _():
                    hop(k, d, up).start()

    for j in range(chunks):
        put(j).wait()
        for d in range(1, owners):
            a2a(d, j).wait_send()
    for k in range(group - 1):
        for d in range(owners):
            for up, goes in ways:

                @pl.when((place - k >= 0 if up else place + k < group) & goes)
                def _():
                    if k == 0 and d == 0:
                        for j in range(chunks):
                            own(j, up).wait_send()
                    else:
                        hop(k, d, up).wait_send()


def cross_kernel(place, windows, data, out):
    group, owners, chunks, _, batch, wins, chans = data.shape
    mine = place[0]
    half = owners * chunks * wins
    for f in range(batch):

        def whitened(b):
            parts = [data[b, :, :, p, f].reshape(half, chans) for p in (0, 1)]
            values = jnp.concatenate(parts, axis=0).astype(F32)
            power = jnp.sum(values * values, axis=0, keepdims=True) * (1.0 / windows)
            return (values * lax.rsqrt(power + eps_power)).astype(BF16)

        right = jnp.concatenate([whitened(b) for b in range(group)], axis=1)
        own = whitened(mine)
        turned = jnp.concatenate([own[half:], -own[:half]], axis=0)
        left = jnp.concatenate([own, turned], axis=1)
        product = lax.dot_general(
            left, right, (((0,), (0,)), ((), ())), preferred_element_type=F32
        )
        scaled = (product * (1.0 / windows)).astype(BF16)
        out[0, f] = scaled[:chans]
        out[1, f] = scaled[chans:]


def local(sizes, traces, offsets, freq_bins, channel_alive):
    chans, wins, seg_len = traces.shape
    owners = sizes["freq"] * sizes["section"]
    group = min(8, sizes["chan"])
    bins = BINS // owners
    chunks = 2
    part = wins // chunks
    rows = 2 * bins * part
    dma = pltpu.SemaphoreType.DMA
    hbm = pl.BlockSpec(memory_space=pl.ANY)
    vmem = pl.BlockSpec(memory_space=pltpu.VMEM)
    gathered = pl.pallas_call(
        functools.partial(gather_kernel, owners, sizes["section"], group),
        in_specs=[pl.BlockSpec(memory_space=pltpu.SMEM), hbm, vmem, vmem, vmem],
        out_specs=hbm,
        out_shape=jax.ShapeDtypeStruct((group, owners, chunks, rows, chans), BF16),
        scratch_shapes=[
            pltpu.VMEM((chunks, chans, part, seg_len), BF16),
            pltpu.VMEM((seg_len // 128, chans * part, 128), F32),
            pltpu.VMEM((2 * BINS * part, chans), F32),
            pltpu.VMEM((chunks, owners, rows, chans), BF16),
            dma((chunks,)),
            dma((chunks,)),
        ]
        + [dma((owners, chunks))] * 2
        + [dma((group, owners, chunks))] * 4,
        compiler_params=pltpu.CompilerParams(collective_id=0, has_side_effects=True),
        name="gather",
    )(
        offsets,
        traces,
        filter_taps(seg_len, TAPS),
        dft_rows(freq_bins, L, owners),
        channel_alive.reshape(1, chans),
    )
    fold = 8
    place = lax.rem(lax.axis_index("chan"), group).astype(jnp.int32).reshape(1)
    return pl.pallas_call(
        lambda place, data, out: cross_kernel(place, wins * owners, data, out),
        grid_spec=pltpu.PrefetchScalarGridSpec(
            num_scalar_prefetch=1,
            grid=(bins // fold,),
            in_specs=[
                pl.BlockSpec(
                    (group, owners, chunks, 2, fold, part, chans),
                    lambda i, _: (0, 0, 0, 0, i, 0, 0),
                )
            ],
            out_specs=pl.BlockSpec((2, fold, chans, group * chans), lambda i, _: (0, i, 0, 0)),
        ),
        out_shape=jax.ShapeDtypeStruct((2, bins, chans, group * chans), BF16),
        name="cross",
    )(place, gathered.reshape(group, owners, chunks, 2, bins, part, chans))


def solution(mesh):
    in_specs = (
        P(("grp", "chan"), ("freq", "section"), None),
        P(("grp", "freq", "section")),
        P(),
        P(("grp", "chan")),
    )
    out_specs = P(None, ("freq", "section"), ("grp", "chan"), None)
    sizes = dict(mesh.shape)
    return jax.shard_map(
        functools.partial(local, sizes),
        mesh=mesh,
        in_specs=in_specs,
        out_specs=out_specs,
        check_vma=False,
    )
```

time: 181 us -> 159 us (0.88)
  Pallas kernels: 170 us -> 156 us
  local copies, waits for them, and re-layouts: 5.64 us -> 0.74 us
  other arithmetic: 4.29 us -> 1.87 us
    pallas_call x1 -> x0, Pallas kernels: 13.3 us -> none  [local(): pl.pallas_call(spectra_kernel, grid_spec=pltpu.PrefetchScalarGridSpec(num...]
    pallas_call x1, Pallas kernels: 15.3 us -> 9.99 us  [local(): pl.pallas_call(lambda place, data, out: cross_kernel(place, wins * owners...]
    unnamed x1 -> x0, local copies, waits for them, and re-layouts: 4.9 us -> none
    pallas_call x1, Pallas kernels: 141 us -> 146 us  [local(): pl.pallas_call(functools.partial(gather_kernel, owners, sizes['section'],...]
    convert_element_type x1 -> x0, other arithmetic: 3.01 us -> none  [toeplitz(): return jnp.where(inside, hann_taper * band_pass, F32(0.0)).astype(BF16)]
where the time goes in v2:
time: 159 us
  Pallas kernels  156 us (98%)
  other arithmetic  1.87 us (1%)
    pallas_call x1, Pallas kernels, local(): pl.pallas_call(functools.partial(gather_kernel, owners, sizes['section'],...  146 us
    pallas_call x1, Pallas kernels, local(): pl.pallas_call(lambda place, data, out: cross_kernel(place, wins * owners...  9.99 us

profile of v2, /device:TPU:0, one launch (start us, length us, event | category | flops | bytes accessed | tf_op | source)
XLA Modules:
  0.0 158.8 jit_solution(8876180672373087355)
XLA Ops:
  0.0 0.6 compare_select_fusion.6.taps
  0.6 0.7 mul.139
  1.3 0.6 cosine_convert_fusion
  1.9 0.7 pad_maximum_fusion
  2.6 146.2 %gather.1 = bf16[4,4,2,1024,128]{4,3,2,1,0:T(8,128)(2,1)} custom-call(s32[32]{0:T(128)} %offsets.1, bf16[128,32,384]{2,1,0:T(8,128)(2,1)} %traces.1, f32[1,384]{1,0:T(1,128)} %compare_select_fusion.6.taps, bf16[256,256]{1,0:T(8,128)(2,1)} %bitcast.7, s32[1,128]{1,0:T(1,128)} %bitcast.8), custom_call_target="tpu_custom_call" | custom-call | tf_op jit(solution)/shard_map/gather/pallas_call | solution.py:275
  148.8 10.0 %cross.1 = bf16[2,32,128,512]{3,2,1,0:T(8,128)(2,1)} custom-call(s32[1]{0:T(128)} %bitcast.place, bf16[4,4,2,2,32,16,128]{6,5,4,3,2,1,0:T(8,128)(2,1)} %bitcast.6), custom_call_target="tpu_custom_call" | custom-call | tf_op jit(solution)/shard_map/cross/pallas_call | solution.py:301

commit v3 on v2

--- a/solution.py
+++ b/solution.py
@@ -237,7 +237,7 @@
                         hop(k, d, up).wait_send()
 
 
-def cross_kernel(place, windows, data, out):
+def cross_kernel(place, windows, data, out, held):
     group, owners, chunks, _, batch, wins, chans = data.shape
     mine = place[0]
     half = owners * chunks * wins
@@ -249,8 +249,11 @@
             power = jnp.sum(values * values, axis=0, keepdims=True) * (1.0 / windows)
             return (values * lax.rsqrt(power + eps_power)).astype(BF16)
 
-        right = jnp.concatenate([whitened(b) for b in range(group)], axis=1)
-        own = whitened(mine)
+        blocks = [whitened(b) for b in range(group)]
+        right = jnp.concatenate(blocks, axis=1)
+        for b in range(group):
+            held[f, b] = blocks[b]
+        own = held[f, mine]
         turned = jnp.concatenate([own[half:], -own[:half]], axis=0)
         left = jnp.concatenate([own, turned], axis=1)
         product = lax.dot_general(
@@ -299,7 +302,7 @@
     fold = 8
     place = lax.rem(lax.axis_index("chan"), group).astype(jnp.int32).reshape(1)
     return pl.pallas_call(
-        lambda place, data, out: cross_kernel(place, wins * owners, data, out),
+        lambda place, *refs: cross_kernel(place, wins * owners, *refs),
         grid_spec=pltpu.PrefetchScalarGridSpec(
             num_scalar_prefetch=1,
             grid=(bins // fold,),
@@ -310,6 +313,7 @@
                 )
             ],
             out_specs=pl.BlockSpec((2, fold, chans, group * chans), lambda i, _: (0, i, 0, 0)),
+            scratch_shapes=[pltpu.VMEM((fold, group, 2 * owners * wins, chans), BF16)],
         ),
         out_shape=jax.ShapeDtypeStruct((2, bins, chans, group * chans), BF16),
         name="cross",

time: 159 us -> 159 us (level)
  no operation moved by 1% of the time
where the time goes in v3:
time: 159 us; the launch traced here: 158 us
  Pallas kernels  156 us (98%)
  other arithmetic  1.87 us (1%)
    pallas_call x1, Pallas kernels, local(): pl.pallas_call(functools.partial(gather_kernel, owners, sizes['section'],...  146 us
    pallas_call x1, Pallas kernels, local(): pl.pallas_call(lambda place, *refs: cross_kernel(place, wins * owners, *r...  9.58 us

profile of v3, /device:TPU:0, one launch (start us, length us, event | category | flops | bytes accessed | tf_op | source)
XLA Modules:
  0.0 158.4 jit_solution(12961298113636880474)
XLA Ops:
  0.0 0.6 compare_select_fusion.6.taps
  0.6 0.7 mul.139
  1.3 0.6 cosine_convert_fusion
  1.9 0.7 pad_maximum_fusion
  2.6 146.2 %gather.1 = bf16[4,4,2,1024,128]{4,3,2,1,0:T(8,128)(2,1)} custom-call(s32[32]{0:T(128)} %offsets.1, bf16[128,32,384]{2,1,0:T(8,128)(2,1)} %traces.1, f32[1,384]{1,0:T(1,128)} %compare_select_fusion.6.taps, bf16[256,256]{1,0:T(8,128)(2,1)} %bitcast.7, s32[1,128]{1,0:T(1,128)} %bitcast.8), custom_call_target="tpu_custom_call" | custom-call | tf_op jit(solution)/shard_map/gather/pallas_call | solution.py:278
  148.8 9.6 %cross.1 = bf16[2,32,128,512]{3,2,1,0:T(8,128)(2,1)} custom-call(s32[1]{0:T(128)} %bitcast.place, bf16[4,4,2,2,32,16,128]{6,5,4,3,2,1,0:T(8,128)(2,1)} %bitcast.6), custom_call_target="tpu_custom_call" | custom-call | tf_op jit(solution)/shard_map/cross/pallas_call | solution.py:304
